TPU v7x, 32 devices: a whole 2x2x4 slice. The times are simulated.
32 devices in a mesh: wide: 8 (over z, y), narrow: 4 (over x, core).
Axes of the slice: x: 2, y: 2, z: 4, core: 2. Of those that a mesh axis runs over, the one named last changes fastest.
Arguments:
- block_input: bfloat16 [8256, 1152], P(('wide', 'narrow')), may hold values from -6 to 6
- skip_input: bfloat16 [8256, 1152], P(('wide', 'narrow')), may hold values from -6 to 6
- out_grad: bfloat16 [8256, 1152], P(('wide', 'narrow')), may hold values from -6 to 6
- skip_weight: bfloat16 [2654208], P(('wide', 'narrow')), may hold values from -0.125 to 0.125
- qkv_weight: bfloat16 [3981312], P(('wide', 'narrow')), may hold values from -0.1875 to 0.1875
- proj_weight: bfloat16 [1327104], P(('wide', 'narrow')), may hold values from -0.5 to 0.5
- up_weight: bfloat16 [5308416], P(('wide', 'narrow')), may hold values from -0.1875 to 0.1875
- down_weight: bfloat16 [5308416], P(('wide', 'narrow')), may hold values from -0.09375 to 0.09375
- gains: float32 [2, 1152], P(None, 'narrow'), may hold values from 0.5 to 1.5
- biases: float32 [5, 1152], P(None, 'narrow'), may hold values from -3 to 3
- up_bias: float32 [4608], P('narrow'), may hold values from -3 to 3
Outputs:
- block_output: bfloat16 [8256, 1152], P(('wide', 'narrow'))
- input_grad: float32 [8256, 1152], P(('wide', 'narrow'))
- skip_grad: float32 [8256, 1152], P(('wide', 'narrow'))
- skip_weight_grad: float32 [2654208], P(('wide', 'narrow'))
- qkv_weight_grad: float32 [3981312], P(('wide', 'narrow'))
- proj_weight_grad: float32 [1327104], P(('wide', 'narrow'))
- up_weight_grad: float32 [5308416], P(('wide', 'narrow'))
- down_weight_grad: float32 [5308416], P(('wide', 'narrow'))
- gains_grad: float32 [2, 1152], P(None, 'narrow')
- biases_grad: float32 [5, 1152], P(None, 'narrow')
- up_bias_grad: float32 [4608], P('narrow')
All inputs are finite; a program needn't handle non-finite values.
Results may differ from a plain program's by a relative error of at most 0.009.
Values may be sent and summed in bfloat16 or wider, within the bound.
No kernel may reach another device: no remote copies, remote signals or barrier semaphores. Data moves between devices by JAX's collectives and lax.ppermute only.
A program may use at most 384 MiB of HBM per device.

v0:
```python
import jax
import jax.numpy as jnp
from jax import lax
from jax.sharding import PartitionSpec as P

HD = 72
SEQ = 258


eps_norm = 1e-05


def layer_norm(values, gain_vec, offset):
    row_mean = jnp.mean(values, axis=-1, keepdims=True)
    centered = values - row_mean
    variance = jnp.mean(centered * centered, axis=-1, keepdims=True)
    return centered * lax.rsqrt(variance + eps_norm) * gain_vec + offset


def exact_gelu(values):
    return jax.nn.gelu(values, approximate=False)


def shaped(gathered, model_width, hidden):
    return (
        gathered[0].reshape(2 * model_width, model_width),
        gathered[1].reshape(model_width, 3 * model_width),
        gathered[2].reshape(model_width, model_width),
        gathered[3].reshape(model_width, hidden),
        gathered[4].reshape(hidden, model_width),
    )


def times_transposed(left, right):
    return jnp.einsum("rf,cf->rc", left, right, preferred_element_type=jnp.float32)


def inner_rows(left, right):
    return jnp.einsum("rc,rd->cd", left, right, preferred_element_type=jnp.float32)


def shards(
    block_input,
    skip_input,
    out_grad,
    skip_weight,
    qkv_weight,
    proj_weight,
    up_weight,
    down_weight,
    gains,
    biases,
    up_bias,
):
    row_count, model_width = block_input.shape
    images_here = row_count // SEQ
    head_count = model_width // HD
    score_scale = HD ** (-0.5)
    gathered = (
        lax.all_gather(skip_weight, ("wide", "narrow"), axis=0, tiled=True),
        lax.all_gather(qkv_weight, ("wide", "narrow"), axis=0, tiled=True),
        lax.all_gather(proj_weight, ("wide", "narrow"), axis=0, tiled=True),
        lax.all_gather(up_weight, ("wide", "narrow"), axis=0, tiled=True),
        lax.all_gather(down_weight, ("wide", "narrow"), axis=0, tiled=True),
    )
    vectors = (
        lax.all_gather(gains, "narrow", axis=1, tiled=True),
        lax.all_gather(biases, "narrow", axis=1, tiled=True),
        lax.all_gather(up_bias, "narrow", axis=0, tiled=True),
    )
    gain_all, bias_all, up_bias_all = vectors
    hidden = up_bias_all.shape[0]
    skip_mat, qkv_mat, proj_mat, up_mat, down_mat = shaped(gathered, model_width, hidden)
    stacked = jnp.concatenate([block_input, skip_input], axis=1)
    joined = jnp.dot(stacked, skip_mat, preferred_element_type=jnp.float32) + bias_all[0]
    normed, norm_back = jax.vjp(layer_norm, joined, gain_all[0], bias_all[1])
    normed_low = normed.astype(jnp.bfloat16)
    projected = jnp.dot(normed_low, qkv_mat, preferred_element_type=jnp.float32).astype(
        jnp.bfloat16
    )
    queries = projected[:, :model_width].reshape(images_here, SEQ, head_count, HD)
    keys_all = projected[:, model_width : 2 * model_width].reshape(images_here, SEQ, head_count, HD)
    values_all = projected[:, 2 * model_width :].reshape(images_here, SEQ, head_count, HD)
    scores = (
        jnp.einsum("iqhd,ikhd->ihqk", queries, keys_all, preferred_element_type=jnp.float32)
        * score_scale
    )
    row_max = jnp.max(scores, axis=-1, keepdims=True)
    exp_scores = jnp.exp(scores - row_max)
    row_sum = jnp.sum(exp_scores, axis=-1, keepdims=True)
    probabilities = exp_scores / row_sum
    row_lse = row_max + jnp.log(row_sum)
    probs_low = probabilities.astype(jnp.bfloat16)
    attended = jnp.einsum(
        "ihqk,ikhd->iqhd", probs_low, values_all, preferred_element_type=jnp.float32
    )
    attended = attended.astype(jnp.bfloat16).reshape(row_count, model_width)
    middle = joined + (
        jnp.dot(attended, proj_mat, preferred_element_type=jnp.float32) + bias_all[2]
    )
    normed_mid, norm_mid_back = jax.vjp(layer_norm, middle, gain_all[1], bias_all[3])
    normed_mid_low = normed_mid.astype(jnp.bfloat16)
    pre_act = jnp.dot(normed_mid_low, up_mat, preferred_element_type=jnp.float32) + up_bias_all
    activated, gelu_back = jax.vjp(exact_gelu, pre_act)
    activated_low = activated.astype(jnp.bfloat16)
    block_output = middle + (
        jnp.dot(activated_low, down_mat, preferred_element_type=jnp.float32) + bias_all[4]
    )
    down_flat = inner_rows(activated_low, out_grad).reshape(-1)
    down_bias_grad = jnp.sum(out_grad.astype(jnp.float32), axis=0)
    activated_grad = times_transposed(out_grad, down_mat)
    pre_grad = gelu_back(activated_grad)[0].astype(jnp.bfloat16)
    up_flat = inner_rows(normed_mid_low, pre_grad).reshape(-1)
    up_bias_grad = jnp.sum(pre_grad.astype(jnp.float32), axis=0)
    normed_mid_grad = times_transposed(pre_grad, up_mat)
    middle_from_norm, gain_mid_grad, offset_mid_grad = norm_mid_back(normed_mid_grad)
    middle_grad = out_grad.astype(jnp.float32) + middle_from_norm
    branch_grad = middle_grad.astype(jnp.bfloat16)
    proj_flat = inner_rows(attended, branch_grad).reshape(-1)
    proj_bias_grad = jnp.sum(branch_grad.astype(jnp.float32), axis=0)
    attended_grad = times_transposed(branch_grad, proj_mat)
    attended_grad = attended_grad.astype(jnp.bfloat16).reshape(images_here, SEQ, head_count, HD)
    scores_again = (
        jnp.einsum("iqhd,ikhd->ihqk", queries, keys_all, preferred_element_type=jnp.float32)
        * score_scale
    )
    probs_again = jnp.exp(scores_again - row_lse)
    probs_again_low = probs_again.astype(jnp.bfloat16)
    prob_grad = jnp.einsum(
        "iqhd,ikhd->ihqk", attended_grad, values_all, preferred_element_type=jnp.float32
    )
    value_grad = jnp.einsum(
        "ihqk,iqhd->ikhd", probs_again_low, attended_grad, preferred_element_type=jnp.float32
    )
    inner_sum = jnp.sum(prob_grad * probs_again, axis=-1, keepdims=True)
    score_grad = (probs_again * (prob_grad - inner_sum)).astype(jnp.bfloat16)
    query_grad = (
        jnp.einsum("ihqk,ikhd->iqhd", score_grad, keys_all, preferred_element_type=jnp.float32)
        * score_scale
    )
    key_grad = (
        jnp.einsum("ihqk,iqhd->ikhd", score_grad, queries, preferred_element_type=jnp.float32)
        * score_scale
    )
    projected_grad = jnp.concatenate(
        [
            query_grad.reshape(row_count, model_width),
            key_grad.reshape(row_count, model_width),
            value_grad.reshape(row_count, model_width),
        ],
        axis=1,
    ).astype(jnp.bfloat16)
    qkv_flat = inner_rows(normed_low, projected_grad).reshape(-1)
    normed_grad = times_transposed(projected_grad, qkv_mat)
    joined_from_norm, gain_first_grad, offset_first_grad = norm_back(normed_grad)
    joined_grad = (middle_grad + joined_from_norm).astype(jnp.bfloat16)
    skip_flat = inner_rows(stacked, joined_grad).reshape(-1)
    skip_bias_grad = jnp.sum(joined_grad.astype(jnp.float32), axis=0)
    both_grads = times_transposed(joined_grad, skip_mat)
    input_grad = both_grads[:, :model_width]
    skip_grad = both_grads[:, model_width:]
    gain_grads = jnp.stack([gain_first_grad, gain_mid_grad])
    bias_grads = jnp.stack(
        [skip_bias_grad, offset_first_grad, proj_bias_grad, offset_mid_grad, down_bias_grad]
    )
    vector_sums = lax.psum((gain_grads, bias_grads, up_bias_grad), ("wide", "narrow"))
    narrow_count = lax.axis_size("narrow")
    place = lax.axis_index("narrow")
    width_part = model_width // narrow_count
    hidden_part = hidden // narrow_count
    gains_grad = lax.dynamic_slice_in_dim(vector_sums[0], place * width_part, width_part, 1)
    biases_grad = lax.dynamic_slice_in_dim(vector_sums[1], place * width_part, width_part, 1)
    up_bias_sum = lax.dynamic_slice_in_dim(vector_sums[2], place * hidden_part, hidden_part, 0)
    matrix_sums = (
        lax.psum_scatter(skip_flat, ("wide", "narrow"), scatter_dimension=0, tiled=True),
        lax.psum_scatter(qkv_flat, ("wide", "narrow"), scatter_dimension=0, tiled=True),
        lax.psum_scatter(proj_flat, ("wide", "narrow"), scatter_dimension=0, tiled=True),
        lax.psum_scatter(up_flat, ("wide", "narrow"), scatter_dimension=0, tiled=True),
        lax.psum_scatter(down_flat, ("wide", "narrow"), scatter_dimension=0, tiled=True),
    )
    return (
        block_output.astype(jnp.bfloat16),
        input_grad,
        skip_grad,
        matrix_sums[0],
        matrix_sums[1],
        matrix_sums[2],
        matrix_sums[3],
        matrix_sums[4],
        gains_grad,
        biases_grad,
        up_bias_sum,
    )


def solution(mesh):
    return jax.shard_map(
        shards,
        mesh=mesh,
        in_specs=(
            P(("wide", "narrow"), None),
            P(("wide", "narrow"), None),
            P(("wide", "narrow"), None),
            P(("wide", "narrow")),
            P(("wide", "narrow")),
            P(("wide", "narrow")),
            P(("wide", "narrow")),
            P(("wide", "narrow")),
            P(None, "narrow"),
            P(None, "narrow"),
            P("narrow"),
        ),
        out_specs=(
            P(("wide", "narrow"), None),
            P(("wide", "narrow"), None),
            P(("wide", "narrow"), None),
            P(("wide", "narrow")),
            P(("wide", "narrow")),
            P(("wide", "narrow")),
            P(("wide", "narrow")),
            P(("wide", "narrow")),
            P(None, "narrow"),
            P(None, "narrow"),
            P("narrow"),
        ),
        check_vma=False,
    )
```

profile of v0, /device:TPU:0, one launch (start us, length us, event | category | flops | bytes accessed | tf_op | source)
XLA Modules:
  0.0 1775.6 jit_solution(2888182057469212620)
XLA Ops:
  35.6 44.2 %all-gather.19.cloned.1.call-done = bf16[32,1,41472]{2,1,0:T(2,128)(2,1)} async-done(((bf16[1,1,41472]{2,1,0:T(2,128)(2,1)}), bf16[32,1,41472]{2,1,0:T(2,128)(2,1)}) %all-gather.19.cloned.1.call-update) | async-done | bytes 2654224 | tf_op jit(solution)/shard_map/all_gather | solution.py:62
  79.8 47.1 %reduce.10 = bf16[32,41472]{1,0:T(8,128)(2,1)S(1)} reduce(bf16[32,1,41472]{2,1,0:T(2,128)(2,1)} %all-gather.19.cloned.1.call-done, bf16[]{:T(256)} %constant.115), dimensions={1}, to_apply=%all-gather.3.reduce_sub_computation | reduce | bytes 5308418 | tf_op jit(solution)/shard_map/all_gather | solution.py:62
  131.9 15.0 all-gather.11.cloned.1.call-done
  146.9 10.8 reshape.227
  162.8 96.7 %all-gather.17.cloned.1.call-done = bf16[32,1,124416]{2,1,0:T(2,128)(2,1)} async-done(((bf16[1,1,124416]{2,1,0:T(2,128)(2,1)}), bf16[32,1,124416]{2,1,0:T(2,128)(2,1)}) %all-gather.17.cloned.1.call-update) | async-done | bytes 7962640 | tf_op jit(solution)/shard_map/all_gather | solution.py:61
  259.5 167.5 %reduce.9 = bf16[32,124416]{1,0:T(8,128)(2,1)} reduce(bf16[32,1,124416]{2,1,0:T(2,128)(2,1)} %all-gather.17.cloned.1.call-done, bf16[]{:T(256)} %constant.115), dimensions={1}, to_apply=%all-gather.2.reduce_sub_computation | reduce | bytes 15925250 | tf_op jit(solution)/shard_map/all_gather | solution.py:61
  427.1 25.9 %reshape.228 = bf16[1152,3456]{1,0:T(8,128)(2,1)} reshape(bf16[32,124416]{1,0:T(8,128)(2,1)} %reduce.9) | data formatting | bytes 15925248 | tf_op jit(solution)/shard_map/reshape | solution.py:27
  472.3 19.1 %reshape.234 = bf16[1152,4608]{1,0:T(8,128)(2,1)} reshape(bf16[5308416]{0:T(1024)(128)(2,1)} %all-gather.13.cloned.1.call-done) | data formatting | bytes 21233664 | tf_op jit(solution)/shard_map/reshape | solution.py:29
  491.4 9.3 convolution_add_fusion
  500.7 20.4 %reshape.235 = bf16[4608,1152]{1,0:T(8,128)(2,1)} reshape(bf16[5308416]{0:T(1024)(128)(2,1)} %all-gather.15.cloned.1.call-done) | data formatting | bytes 21233664 | tf_op jit(solution)/shard_map/reshape | solution.py:30
  521.2 18.1 %convert_reduce_fusion = (f32[4608]{0:T(1024)S(1)}, bf16[258,4608]{1,0:T(8,128)(2,1)S(1)}, f32[258,4608]{1,0:T(8,128)}) fusion(f32[258,4608]{1,0:T(8,128)} %convolution_add_fusion, bf16[258,1152]{1,0:T(8,128)(2,1)S(1)} %copy-done.13, bf16[4608,1152]{1,0:T(8,128)(2,1)} %reshape.235), kind=kOutput, calls=%fused_computation.11 | convolution fusion | flops 2827113984 | bytes 23118336 | tf_op jit(solution)/shard_map/rf,cf->rc/dot_general | solution.py:35
  539.2 8.4 multiply_reduce_fusion.2
  571.9 8.5 multiply_reduce_fusion.3
  580.4 10.7 fusion.20
  591.1 10.5 fusion.29
  614.2 8.4 fusion.39
  622.6 11.2 reshape.240
  633.8 16.7 reshape.241
  650.5 20.9 %reshape.243 = f32[5308416]{0:T(1024)} reshape(f32[1152,4608]{1,0:T(8,128)} %fusion.29) | data formatting | bytes 42467328 | tf_op jit(solution)/shard_map/reshape | solution.py:113
  671.4 12.5 fusion.41
  683.9 22.0 %reshape.244 = f32[5308416]{0:T(1024)} reshape(f32[4608,1152]{1,0:T(8,128)} %fusion.41) | data formatting | bytes 42467328 | tf_op jit(solution)/shard_map/reshape | solution.py:109
  706.0 41.9 %all-reduce.5 = (f32[2,1152]{1,0:T(2,128)S(1)}, f32[5,1152]{1,0:T(8,128)S(1)}, f32[4608]{0:T(1024)S(1)}) all-reduce(f32[2,1152]{1,0:T(2,128)S(1)} %pad_maximum_fusion.3, f32[5,1152]{1,0:T(8,128)S(1)} %stack.23, f32[4608]{0:T(1024)S(1)} %get-tuple-element.32), channel_id=1, replica_groups=mesh['wide'=8,'narrow'=4] {'wide','narrow'}, use_global_device_ids=true, to_apply=%region_18.0 | all-reduce | flops 12672 | bytes 101376 | tf_op jit(solution)/shard_map/psum | solution.py:166
  757.0 7.5 fusion.15
  764.5 994.6 %all-reduce.9.cloned.1.call-done = (f32[2654208]{0:T(1024)}, f32[3981312]{0:T(1024)}, f32[1327104]{0:T(1024)}, f32[5308416]{0:T(1024)}, f32[5308416]{0:T(1024)}) async-done(((f32[2654208]{0:T(1024)}, f32[3981312]{0:T(1024)}, f32[1327104]{0:T(1024)}, f32[5308416]{0:T(1024)}, f32[5308416]{0:T(1024)}), (f32[2654208]{0:T(1024)}, f32[3981312]{0:T(1024)}, f32[1327104]{0:T(1024)}, f32[5308416]{0:T(1024)}, ...) | async-done | bytes 74317840
  (146 shorter events, 112.9 us)
Async XLA Ops:
  7.2 72.6 %all-gather.19.cloned.1.call-start = ((), (), s32[]{:S(2)}) async-start(), calls=%async_computation.4 | async-start | bytes 5474304 | tf_op jit(solution)/shard_map/all_gather | solution.py:62
  8.9 138.0 %all-gather.11.cloned.1.call-start = ((), (), s32[]{:S(2)}) async-start(), calls=%async_computation | async-start | bytes 5474304 | tf_op jit(solution)/shard_map/all_gather | solution.py:60
  9.6 249.9 %all-gather.17.cloned.1.call-start = ((), (), s32[]{:S(2)}) async-start(), calls=%async_computation.3 | async-start | bytes 16422912 | tf_op jit(solution)/shard_map/all_gather | solution.py:61
  11.7 460.6 %all-gather.13.cloned.1.call-start = ((), (), s32[]{:S(2)}) async-start(), calls=%async_computation.1 | async-start | bytes 10948608 | tf_op jit(solution)/shard_map/all_gather | solution.py:63
  12.3 488.4 %all-gather.15.cloned.1.call-start = ((), (), s32[]{:S(2)}) async-start(), calls=%async_computation.2 | async-start | bytes 10948608 | tf_op jit(solution)/shard_map/all_gather | solution.py:64
  12.9 1746.2 %all-reduce.9.cloned.1.call-start = ((), (), s32[]{:S(2)}) async-start(), calls=%async_computation.5 | async-start | bytes 148635648
  162.8 264.2 %copy-start.20 = (f32[258]{0:T(512)}, f32[258]{0:T(512)S(1)}, u32[]{:S(2)}) copy-start(f32[258]{0:T(512)S(1)} %multiply_reduce_fusion.7) | copy-start | bytes 3100
  460.6 5.8 copy-start.7
  462.4 4.0 copy-start.9
  471.9 75.7 %copy-start.1 = (f32[258,1152]{1,0:T(8,128)}, f32[258,1152]{1,0:T(8,128)S(1)}, u32[]{:S(2)}) copy-start(f32[258,1152]{1,0:T(8,128)S(1)} %get-tuple-element.54) | copy-start | bytes 3566596
  500.7 20.4 %copy-start.13 = (bf16[258,1152]{1,0:T(8,128)(2,1)S(1)}, bf16[258,1152]{1,0:T(8,128)(2,1)}, u32[]{:S(2)}) copy-start(bf16[258,1152]{1,0:T(8,128)(2,1)} %param.13) | copy-start | bytes 1783300
  539.2 8.4 copy-start.18
  555.3 6.2 copy-start.17
  556.2 10.4 slice-start
  561.5 5.1 slice-start.1
  568.3 3.6 copy-start.15
  580.4 10.7 copy-start.2
  580.4 10.7 copy-start.19
  580.4 21.2 %slice-start.2 = ((s8[4866048]{0:T(1024)(128)(4,1)}), s8[4194304]{0:T(1024)(128)(4,1)S(1)}, s32[]{:S(2)}) async-start(s8[4866048]{0:T(1024)(128)(4,1)} %bitcast.80), calls=%async_computation.8 | async-start | bytes 8388608
  580.4 21.2 %slice-start.4 = ((s8[4866048]{0:T(1024)(128)(4,1)}), s8[4194304]{0:T(1024)(128)(4,1)S(1)}, s32[]{:S(2)}) async-start(s8[4866048]{0:T(1024)(128)(4,1)} %bitcast.82), calls=%async_computation.10 | async-start | bytes 8388608
  591.1 10.5 slice-start.3
  591.1 10.5 slice-start.5
  603.9 6.8 copy-start.21
  603.9 8.6 copy-start.14
  (11 other events, 23.4 us)
Sparse Core Ops, SparseCore 0:
  11.5 68.2 all-gather.18
  82.7 64.0 all-gather.10
  150.4 109.1 all-gather.16
  262.3 84.8 all-gather.12
  350.0 85.1 all-gather.14
  706.0 1053.0 all-reduce.8
where the time goes:
time: 1780 us
  waiting for transfers between devices  1150 us (65%)
  other arithmetic  225 us (13%)
  local copies, waits for them, and re-layouts  192 us (11%)
  matrix products  132 us (7%)
  blocking collectives  59.1 us (3%)
    unnamed x7, waiting for transfers between devices  996 us
    all_gather x1, other arithmetic, shards(): lax.all_gather(qkv_weight, ('wide', 'narrow'), axis=0, tiled=True)  168 us
    all_gather x1, waiting for transfers between devices, shards(): lax.all_gather(qkv_weight, ('wide', 'narrow'), axis=0, tiled=True)  96.7 us
    all_gather x1, other arithmetic, shards(): lax.all_gather(proj_weight, ('wide', 'narrow'), axis=0, tiled=True)  47.1 us
    dot_general x5, matrix products, inner_rows(): jnp.einsum('rc,rd->cd', left, right, preferred_element_type=jnp.float32)  46 us
    all_gather x1, waiting for transfers between devices, shards(): lax.all_gather(proj_weight, ('wide', 'narrow'), axis=0, tiled=True)  44.2 us
    psum x1, blocking collectives, shards(): lax.psum((gain_grads, bias_grads, up_bias_grad), ('wide', 'narrow'))  41.9 us
    dot_general x5, matrix products, times_transposed(): jnp.einsum('rf,cf->rc', left, right, preferred_element_type=jnp.float32)  40.5 us
  transfers between devices with their start and end apart: 6, of which 4 were waited for; matrix products, arithmetic and copies ran while one was open for 19% of the time, Pallas kernels for 0%

commit v1 on v0

--- a/solution.py
+++ b/solution.py
@@ -1,6 +1,11 @@
+import functools
+import math
+
 import jax
 import jax.numpy as jnp
 from jax import lax
+from jax.experimental import pallas as pl
+from jax.experimental.pallas import tpu as pltpu
 from jax.sharding import PartitionSpec as P
 
 HD = 72
@@ -193,9 +198,401 @@
     )
 
 
+AXES = ("wide", "narrow")
+DEVICES = 32
+
+
+def flipped(bits_core0, bits_core1):
+    return [
+        (device, device ^ (bits_core1 if device & 1 else bits_core0)) for device in range(DEVICES)
+    ]
+
+
+TO_CORE = flipped(1, 1)
+TO_Z = [flipped(8 * step, 8 * step) for step in range(4)]
+TO_NEAR = flipped(4, 2)
+TO_FAR = flipped(2, 4)
+TO_X = flipped(2, 2)
+TO_Y = flipped(4, 4)
+
+
+def send(value, pairs):
+    return lax.ppermute(value, AXES, pairs)
+
+
+def places():
+    device = lax.axis_index("wide") * 4 + lax.axis_index("narrow")
+    core = device & 1
+    return device, core
+
+
+def spread(block):
+    group = jnp.stack([block] + [send(block, TO_Z[step]) for step in (1, 2, 3)])
+    group = jnp.concatenate([group, send(group, TO_NEAR)], 0)
+    other = send(group, TO_FAR)
+    return group, other, send(group, TO_CORE), send(other, TO_CORE)
+
+
+def gather_copies(by_rows, pieces, held, sems):
+    device = lax.axis_index("wide") * 4 + lax.axis_index("narrow")
+    core = device % 2
+    chip = device // 2
+    z, y, x = chip // 4, (chip // 2) % 2, chip % 2
+    own, theirs = pieces[:2], pieces[2:]
+    part = pieces[0].shape[-1]
+    rest = held.shape[-1] - part
+    copies = []
+    for far in range(2):
+        for near in range(2):
+            flip_y = near * (1 - core) + far * core
+            flip_x = far * (1 - core) + near * core
+            corner = ((y + flip_y) % 2) * 2 + (x + flip_x) % 2
+            for step in range(4):
+                z_high, z_low = z // 2, z % 2
+                z_high = 1 - z_high if step & 2 else z_high
+                z_low = 1 - z_low if step & 1 else z_low
+                place = (z_high * 2 + z_low) * 4 + corner
+                mine = own[far].at[near * 4 + step]
+                other = theirs[near].at[far * 4 + step]
+                if by_rows:
+                    to_mine = held.at[place, core]
+                    to_other = held.at[place, 1 - core]
+                else:
+                    from_other = pl.multiple_of((1 - core) * (part - rest), 128)
+                    other = other.at[:, pl.ds(from_other, rest)]
+                    to_mine = held.at[place, :, pl.ds(pl.multiple_of(core * rest, 128), part)]
+                    to_other = held.at[
+                        place, :, pl.ds(pl.multiple_of((1 - core) * part, 128), rest)
+                    ]
+                n = 2 * len(copies)
+                copies.append(
+                    (
+                        place,
+                        pltpu.make_async_copy(mine, to_mine, sems.at[n]),
+                        pltpu.make_async_copy(other, to_other, sems.at[n + 1]),
+                    )
+                )
+    return copies
+
+
+def assemble_kernel(by_rows, *refs):
+    pieces, (out_ref, held, sem_in, sem_out) = refs[:4], refs[4:]
+    copies = gather_copies(by_rows, pieces, held, sem_in)
+    for _, mine, other in copies:
+        mine.start()
+        other.start()
+    outs = []
+    for n, (place, mine, other) in enumerate(copies):
+        mine.wait()
+        other.wait()
+        out = pltpu.make_async_copy(held.at[place], out_ref.at[place], sem_out.at[n])
+        out.start()
+        outs.append(out)
+    for out in outs:
+        out.wait()
+
+
+def assemble(pieces, rows, width, by_rows):
+    shape = (16, 2, rows, width) if by_rows else (16, rows, width)
+    size = 2 * math.prod(shape)
+    out = pl.pallas_call(
+        functools.partial(assemble_kernel, by_rows),
+        out_shape=jax.ShapeDtypeStruct(shape, jnp.bfloat16),
+        in_specs=[pl.BlockSpec(memory_space=pl.ANY)] * 4,
+        out_specs=pl.BlockSpec(memory_space=pl.ANY),
+        scratch_shapes=[
+            pltpu.VMEM(shape, jnp.bfloat16),
+            pltpu.SemaphoreType.DMA((32,)),
+            pltpu.SemaphoreType.DMA((16,)),
+        ],
+        cost_estimate=pl.CostEstimate(flops=0, bytes_accessed=2 * size, transcendentals=0),
+        name="assemble",
+    )(*pieces)
+    return out.reshape(-1, width)
+
+
+def fold(kept, sent_to_core, chip, core):
+    f32 = jnp.float32
+    bf16 = jnp.bfloat16
+    corner = chip % 4
+    z = chip // 4
+    near_bit = 2 - core
+    far_bit = 1 + core
+    from_core = send(sent_to_core, TO_CORE)
+
+    def at(bits):
+        blocks = lax.dynamic_index_in_dim(from_core, corner ^ bits, 1, keepdims=False)
+        return kept(0, 4, corner ^ bits).astype(f32) + blocks.astype(f32)
+
+    to_far = jnp.stack([at(far_bit), at(far_bit | near_bit)]).astype(bf16)
+    from_far = send(to_far, TO_FAR)
+    to_near = (at(near_bit) + from_far[1].astype(f32)).astype(bf16)
+    from_near = send(to_near, TO_NEAR)
+
+    def total(place):
+        blocks = [
+            kept(place, 1, corner)[0],
+            lax.dynamic_slice(
+                from_core, (place, corner, 0, 0), (1, 1) + from_core.shape[2:]
+            )[0, 0],
+            lax.dynamic_index_in_dim(from_far[0], place, 0, keepdims=False),
+            lax.dynamic_index_in_dim(from_near, place, 0, keepdims=False),
+        ]
+        blocks = [b.astype(f32) for b in blocks]
+        return (blocks[0] + blocks[1]) + (blocks[2] + blocks[3])
+
+    arrived = [send(total(z ^ step).astype(bf16), TO_Z[step]) for step in (1, 2, 3)]
+    return total(z) + sum(a.astype(f32) for a in arrived)
+
+
+def fold_rows(blocks, chip, core):
+    def kept(start, count, corner):
+        shape = (count, 1, 1) + blocks.shape[3:]
+        return lax.dynamic_slice(blocks, (start, corner, core, 0, 0), shape)[:, 0, 0]
+
+    theirs = lax.dynamic_index_in_dim(blocks, 1 - core, 2, keepdims=False)
+    return fold(kept, theirs, chip, core).reshape(-1)
+
+
+def half_columns(array, whose, part):
+    start = whose * (array.shape[1] - part)
+    return lax.dynamic_slice_in_dim(array, start, part, 1)
+
+
+def join_columns(summed, core, width, rows):
+    part = summed.shape[1]
+    mine = lax.dynamic_slice_in_dim(summed, core * rows, rows, 0)
+    other = send(lax.dynamic_slice_in_dim(summed, (1 - core) * rows, rows, 0), TO_CORE)
+    rest = width - part
+    first = jnp.concatenate([mine, other[:, part - rest :]], 1)
+    second = jnp.concatenate([other[:, :rest], mine], 1)
+    return jnp.where(core == 0, first, second).reshape(-1)
+
+
+def gathered_vectors(gains, biases, up_bias, core, x):
+    flat = jnp.concatenate([gains.reshape(-1), biases.reshape(-1), up_bias])[None]
+
+    def both(mine, other, place):
+        return jnp.where(
+            place == 0, jnp.concatenate([mine, other], 0), jnp.concatenate([other, mine], 0)
+        )
+
+    flat = both(flat, send(flat, TO_CORE), core)
+    everyone = both(flat, send(flat, TO_X), x)
+    width = gains.shape[1]
+    gain_all = everyone[:, : 2 * width].reshape(4, 2, width).transpose(1, 0, 2).reshape(2, 4 * width)
+    bias_all = (
+        everyone[:, 2 * width : 7 * width].reshape(4, 5, width).transpose(1, 0, 2).reshape(5, 4 * width)
+    )
+    return gain_all, bias_all, everyone[:, 7 * width :].reshape(-1)
+
+
+def vector_total(gain_grads, bias_grads, up_bias_grad, device):
+    width = gain_grads.shape[1] // 4
+    rows = jnp.concatenate([gain_grads, bias_grads], 0).reshape(7, 4, width).transpose(1, 0, 2)
+    packed = jnp.concatenate([rows.reshape(4, 7 * width), up_bias_grad.reshape(4, -1)], 1)
+    core = device & 1
+    x = (device >> 1) & 1
+    packed = packed.reshape(2, 2, -1)
+
+    def take(array, index, dim):
+        return lax.dynamic_index_in_dim(array, index, dim, keepdims=False)
+
+    packed = take(packed, core, 1) + send(take(packed, 1 - core, 1), TO_CORE)
+    packed = take(packed, x, 0) + send(take(packed, 1 - x, 0), TO_X)
+    for pairs in (TO_Y, TO_Z[1], TO_Z[2]):
+        packed = packed + send(packed, pairs)
+    return (
+        packed[: 2 * width].reshape(2, width),
+        packed[2 * width : 7 * width].reshape(5, width),
+        packed[7 * width :],
+    )
+
+
+def padded_half(width):
+    return -(-width // 256) * 128
+
+
+def fast_shards(
+    block_input,
+    skip_input,
+    out_grad,
+    skip_weight,
+    qkv_weight,
+    proj_weight,
+    up_weight,
+    down_weight,
+    gains,
+    biases,
+    up_bias,
+):
+    row_count, model_width = block_input.shape
+    hidden = 4 * up_bias.shape[0]
+    device, core = places()
+    chip = device // 2
+    images_here = row_count // SEQ
+    head_count = model_width // HD
+    score_scale = HD ** (-0.5)
+    bf16 = jnp.bfloat16
+
+    gain_all, bias_all, up_bias_all = gathered_vectors(gains, biases, up_bias, core, chip % 2)
+    rows = model_width // DEVICES
+    skip_pieces = spread(skip_weight.reshape(2 * rows, model_width))
+    wide_mats = [
+        qkv_weight.reshape(rows, 3 * model_width),
+        proj_weight.reshape(rows, model_width),
+        up_weight.reshape(rows, hidden),
+    ]
+    parts = [padded_half(m.shape[1]) for m in wide_mats]
+    mine = jnp.concatenate([half_columns(m, core, p) for m, p in zip(wide_mats, parts)], 1)
+    others = send(
+        jnp.concatenate([half_columns(m, 1 - core, p) for m, p in zip(wide_mats, parts)], 1), TO_CORE
+    )
+    chip_rows = jnp.where(
+        core == 0, jnp.concatenate([mine, others], 0), jnp.concatenate([others, mine], 0)
+    )
+    qkv_pieces = spread(chip_rows[:, : parts[0]])
+    proj_pieces = spread(chip_rows[:, parts[0] : parts[0] + parts[1]])
+    up_pieces = spread(chip_rows[:, parts[0] + parts[1] :])
+    down_pieces = spread(down_weight.reshape(4 * rows, model_width))
+
+    skip_mat = assemble(skip_pieces, 2 * rows, model_width, True)
+    qkv_mat = assemble(qkv_pieces, 2 * rows, 3 * model_width, False)
+    proj_mat = assemble(proj_pieces, 2 * rows, model_width, False)
+    up_mat = assemble(up_pieces, 2 * rows, hidden, False)
+    down_mat = assemble(down_pieces, 4 * rows, model_width, True)
+
+    stacked = jnp.concatenate([block_input, skip_input], axis=1)
+    joined = jnp.dot(stacked, skip_mat, preferred_element_type=jnp.float32) + bias_all[0]
+    normed, norm_back = jax.vjp(layer_norm, joined, gain_all[0], bias_all[1])
+    normed_low = normed.astype(bf16)
+    projected = jnp.dot(normed_low, qkv_mat, preferred_element_type=jnp.float32).astype(bf16)
+    queries = projected[:, :model_width].reshape(images_here, SEQ, head_count, HD)
+    keys_all = projected[:, model_width : 2 * model_width].reshape(images_here, SEQ, head_count, HD)
+    values_all = projected[:, 2 * model_width :].reshape(images_here, SEQ, head_count, HD)
+    scores = (
+        jnp.einsum("iqhd,ikhd->ihqk", queries, keys_all, preferred_element_type=jnp.float32)
+        * score_scale
+    )
+    row_max = jnp.max(scores, axis=-1, keepdims=True)
+    exp_scores = jnp.exp(scores - row_max)
+    row_sum = jnp.sum(exp_scores, axis=-1, keepdims=True)
+    probabilities = exp_scores / row_sum
+    row_lse = row_max + jnp.log(row_sum)
+    probs_low = probabilities.astype(bf16)
+    attended = jnp.einsum(
+        "ihqk,ikhd->iqhd", probs_low, values_all, preferred_element_type=jnp.float32
+    )
+    attended = attended.astype(bf16).reshape(row_count, model_width)
+    middle = joined + (
+        jnp.dot(attended, proj_mat, preferred_element_type=jnp.float32) + bias_all[2]
+    )
+    normed_mid, norm_mid_back = jax.vjp(layer_norm, middle, gain_all[1], bias_all[3])
+    normed_mid_low = normed_mid.astype(bf16)
+    pre_act = jnp.dot(normed_mid_low, up_mat, preferred_element_type=jnp.float32) + up_bias_all
+    activated, gelu_back = jax.vjp(exact_gelu, pre_act)
+    activated_low = activated.astype(bf16)
+
+    down_blocks = inner_rows(activated_low, out_grad).astype(bf16).reshape(4, 4, 2, 4 * rows, model_width)
+    down_total = fold_rows(down_blocks, chip, core)
+    block_output = middle + (
+        jnp.dot(activated_low, down_mat, preferred_element_type=jnp.float32) + bias_all[4]
+    )
+    down_bias_grad = jnp.sum(out_grad.astype(jnp.float32), axis=0)
+    activated_grad = times_transposed(out_grad, down_mat)
+    pre_grad = gelu_back(activated_grad)[0].astype(bf16)
+
+    def by_columns(left, right, part):
+        def one(whose):
+            return (
+                inner_rows(left, half_columns(right, whose, part))
+                .astype(bf16)
+                .reshape(4, 4, 2 * rows, part)
+            )
+
+        width = right.shape[1]
+        theirs = one(1 - core)
+        mine = one(core)
+
+        def kept(start, count, corner):
+            return lax.dynamic_slice(mine, (start, corner, 0, 0), (count, 1) + mine.shape[2:])[:, 0]
+
+        return join_columns(fold(kept, theirs, chip, core), core, width, rows)
+
+    up_total = by_columns(normed_mid_low, pre_grad, parts[2])
+    up_bias_grad = jnp.sum(pre_grad.astype(jnp.float32), axis=0)
+    normed_mid_grad = times_transposed(pre_grad, up_mat)
+    middle_from_norm, gain_mid_grad, offset_mid_grad = norm_mid_back(normed_mid_grad)
+    middle_grad = out_grad.astype(jnp.float32) + middle_from_norm
+    branch_grad = middle_grad.astype(bf16)
+    proj_total = by_columns(attended, branch_grad, parts[1])
+    proj_bias_grad = jnp.sum(branch_grad.astype(jnp.float32), axis=0)
+    attended_grad = times_transposed(branch_grad, proj_mat)
+    attended_grad = attended_grad.astype(bf16).reshape(images_here, SEQ, head_count, HD)
+    scores_again = (
+        jnp.einsum("iqhd,ikhd->ihqk", queries, keys_all, preferred_element_type=jnp.float32)
+        * score_scale
+    )
+    probs_again = jnp.exp(scores_again - row_lse)
+    probs_again_low = probs_again.astype(bf16)
+    prob_grad = jnp.einsum(
+        "iqhd,ikhd->ihqk", attended_grad, values_all, preferred_element_type=jnp.float32
+    )
+    value_grad = jnp.einsum(
+        "ihqk,iqhd->ikhd", probs_again_low, attended_grad, preferred_element_type=jnp.float32
+    )
+    inner_sum = jnp.sum(prob_grad * probs_again, axis=-1, keepdims=True)
+    score_grad = (probs_again * (prob_grad - inner_sum)).astype(bf16)
+    query_grad = (
+        jnp.einsum("ihqk,ikhd->iqhd", score_grad, keys_all, preferred_element_type=jnp.float32)
+        * score_scale
+    )
+    key_grad = (
+        jnp.einsum("ihqk,iqhd->ikhd", score_grad, queries, preferred_element_type=jnp.float32)
+        * score_scale
+    )
+    projected_grad = jnp.concatenate(
+        [
+            query_grad.reshape(row_count, model_width),
+            key_grad.reshape(row_count, model_width),
+            value_grad.reshape(row_count, model_width),
+        ],
+        axis=1,
+    ).astype(bf16)
+    qkv_total = by_columns(normed_low, projected_grad, parts[0])
+    normed_grad = times_transposed(projected_grad, qkv_mat)
+    joined_from_norm, gain_first_grad, offset_first_grad = norm_back(normed_grad)
+    joined_grad = (middle_grad + joined_from_norm).astype(bf16)
+    skip_blocks = inner_rows(stacked, joined_grad).astype(bf16).reshape(4, 4, 2, 2 * rows, model_width)
+    skip_total = fold_rows(skip_blocks, chip, core)
+    skip_bias_grad = jnp.sum(joined_grad.astype(jnp.float32), axis=0)
+    both_grads = times_transposed(joined_grad, skip_mat)
+    input_grad = both_grads[:, :model_width]
+    skip_grad = both_grads[:, model_width:]
+    gain_grads = jnp.stack([gain_first_grad, gain_mid_grad])
+    bias_grads = jnp.stack(
+        [skip_bias_grad, offset_first_grad, proj_bias_grad, offset_mid_grad, down_bias_grad]
+    )
+    gains_grad, biases_grad, up_bias_total = vector_total(gain_grads, bias_grads, up_bias_grad, device)
+    return (
+        block_output.astype(bf16),
+        input_grad,
+        skip_grad,
+        skip_total,
+        qkv_total,
+        proj_total,
+        up_total,
+        down_total,
+        gains_grad,
+        biases_grad,
+        up_bias_total,
+    )
+
+
 def solution(mesh):
+    fast = dict(mesh.shape) == {"wide": 8, "narrow": 4}
     return jax.shard_map(
-        shards,
+        fast_shards if fast else shards,
         mesh=mesh,
         in_specs=(
             P(("wide", "narrow"), None),

time: 1780 us -> 643 us (0.36)
  waiting for transfers between devices: 1150 us -> 267 us
  other arithmetic: 225 us -> 57.5 us
  local copies, waits for them, and re-layouts: 192 us -> 65.1 us
  starting transfers between devices: 0.24 us -> 98.2 us
  blocking collectives: 59.1 us -> 0 us
  Pallas kernels: 0 us -> 31.6 us
  matrix products: 132 us -> 111 us
    unnamed x7 -> x0, waiting for transfers between devices: 996 us -> none
    ppermute x0 -> x76, waiting for transfers between devices: none -> 267 us  [send(): return lax.ppermute(value, AXES, pairs)]
    all_gather x3 -> x0, other arithmetic: 215 us -> none  [the longest x1 168 us: shards(): lax.all_gather(qkv_weight, ('wide', 'narrow'), axis=0, tiled=True)]
    all_gather x5 -> x0, waiting for transfers between devices: 156 us -> none  [the longest x1 96.7 us: shards(): lax.all_gather(qkv_weight, ('wide', 'narrow'), axis=0, tiled=True)]
    reshape x15 -> x11, local copies, waits for them, and re-layouts: 161 us -> 9.93 us  [the longest x1 2.1 us: fast_shards(): down_pieces = spread(down_weight.reshape(4 * rows, model_width))]
    ppermute x0 -> x76, starting transfers between devices: none -> 98.2 us  [send(): return lax.ppermute(value, AXES, pairs)]
    psum x1 -> x0, blocking collectives: 41.9 us -> none  [shards(): lax.psum((gain_grads, bias_grads, up_bias_grad), ('wide', 'narrow'))]
    pallas_call x0 -> x5, Pallas kernels: none -> 31.6 us  [assemble(): pl.pallas_call(functools.partial(assemble_kernel, by_rows), out_shape=jax...]
  transfers between devices with their start and end apart: 6 -> 76, of which waited for: 4 -> 31; matrix products, arithmetic and copies ran while one was open for 19% -> 24% of each run, Pallas kernels for 0% -> 4%
where the time goes in v1:
time: 643 us; the launch traced here: 633 us
  waiting for transfers between devices  267 us (42%)
  matrix products  111 us (17%)
  starting transfers between devices  98.2 us (15%)
  local copies, waits for them, and re-layouts  65.1 us (10%)
  other arithmetic  57.5 us (9%)
  Pallas kernels  31.6 us (5%)
    ppermute x76, waiting for transfers between devices, send(): return lax.ppermute(value, AXES, pairs)  267 us
    ppermute x76, starting transfers between devices, send(): return lax.ppermute(value, AXES, pairs)  98.2 us
    dot_general x8, matrix products, inner_rows(): jnp.einsum('rc,rd->cd', left, right, preferred_element_type=jnp.float32)  33.7 us
    pallas_call x5, Pallas kernels, assemble(): pl.pallas_call(functools.partial(assemble_kernel, by_rows), out_shape=jax...  31.6 us
    dot_general x5, matrix products, times_transposed(): jnp.einsum('rf,cf->rc', left, right, preferred_element_type=jnp.float32)  26.8 us
    unnamed x168, local copies, waits for them, and re-layouts  21.5 us
    dot_general x1, matrix products, fast_shards(): jnp.dot(normed_mid_low, up_mat, preferred_element_type=jnp.float32)  17.9 us
    convert_element_type x5, other arithmetic, fold(): to_near = (at(near_bit) + from_far[1].astype(f32)).astype(bf16)  14 us
  transfers between devices with their start and end apart: 76, of which 31 were waited for; matrix products, arithmetic and copies ran while one was open for 24% of the time, Pallas kernels for 4%

profile of v1, /device:TPU:0, one launch (start us, length us, event | category | flops | bytes accessed | tf_op | source)
XLA Modules:
  0.0 632.8 jit_solution(15151193930520267318)
XLA Ops:
  23.4 13.6 %collective-permute-done.1 = bf16[72,1152]{1,0:T(8,128)(2,1)S(1)} collective-permute-done((bf16[72,1152]{1,0:T(8,128)(2,1)}, bf16[72,1152]{1,0:T(8,128)(2,1)S(1)}, u32[]{:S(2)}, u32[]{:S(2)}) %collective-permute-start.1) | collective-permute-done | bytes 165920 | tf_op jit(solution)/shard_map/ppermute | solution.py:220
  38.7 11.5 %collective-permute-done.32 = bf16[144,1152]{1,0:T(8,128)(2,1)S(1)} collective-permute-done((bf16[144,1152]{1,0:T(8,128)(2,1)}, bf16[144,1152]{1,0:T(8,128)(2,1)S(1)}, u32[]{:S(2)}, u32[]{:S(2)}) %collective-permute-start.32) | collective-permute-done | bytes 331808 | tf_op jit(solution)/shard_map/ppermute | solution.py:220
  66.3 8.7 %collective-permute-done.10 = bf16[72,1792]{1,0:T(8,128)(2,1)S(1)} collective-permute-done((bf16[72,1792]{1,0:T(8,128)(2,1)S(1)}, bf16[72,1792]{1,0:T(8,128)(2,1)S(1)}, u32[]{:S(2)}, u32[]{:S(2)}) %collective-permute-start.10) | collective-permute-done | bytes 258080 | tf_op jit(solution)/shard_map/ppermute | solution.py:220
  78.6 10.8 %collective-permute-done.11 = bf16[72,1792]{1,0:T(8,128)(2,1)S(1)} collective-permute-done((bf16[72,1792]{1,0:T(8,128)(2,1)S(1)}, bf16[72,1792]{1,0:T(8,128)(2,1)S(1)}, u32[]{:S(2)}, u32[]{:S(2)}) %collective-permute-start.11) | collective-permute-done | bytes 258080 | tf_op jit(solution)/shard_map/ppermute | solution.py:220
  92.0 17.7 %collective-permute-done.24 = bf16[72,2304]{1,0:T(8,128)(2,1)S(1)} collective-permute-done((bf16[72,2304]{1,0:T(8,128)(2,1)S(1)}, bf16[72,2304]{1,0:T(8,128)(2,1)S(1)}, u32[]{:S(2)}, u32[]{:S(2)}) %collective-permute-start.24) | collective-permute-done | bytes 331808 | tf_op jit(solution)/shard_map/ppermute | solution.py:220
  121.7 16.6 %collective-permute-done.13 = bf16[4,72,1792]{2,1,0:T(8,128)(2,1)S(1)} collective-permute-done((bf16[4,72,1792]{2,1,0:T(8,128)(2,1)S(1)}, bf16[4,72,1792]{2,1,0:T(8,128)(2,1)S(1)}, u32[]{:S(2)}, u32[]{:S(2)}) %collective-permute-start.13) | collective-permute-done | bytes 1032224 | tf_op jit(solution)/shard_map/ppermute | solution.py:220
  150.1 22.4 %collective-permute-done.27 = bf16[4,72,2304]{2,1,0:T(8,128)(2,1)S(1)} collective-permute-done((bf16[4,72,2304]{2,1,0:T(8,128)(2,1)S(1)}, bf16[4,72,2304]{2,1,0:T(8,128)(2,1)S(1)}, u32[]{:S(2)}, u32[]{:S(2)}) %collective-permute-start.27) | collective-permute-done | bytes 1327136 | tf_op jit(solution)/shard_map/ppermute | solution.py:220
  175.8 10.7 %collective-permute-done.4.refs_1_ = bf16[8,72,1152]{2,1,0:T(8,128)(2,1)} collective-permute-done((bf16[8,72,1152]{2,1,0:T(8,128)(2,1)S(1)}, bf16[8,72,1152]{2,1,0:T(8,128)(2,1)}, u32[]{:S(2)}, u32[]{:S(2)}) %collective-permute-start.4) | collective-permute-done | bytes 1327136 | tf_op jit(solution)/shard_map/ppermute | solution.py:220
  186.5 9.7 %collective-permute-start.6 = (bf16[8,72,1152]{2,1,0:T(8,128)(2,1)}, bf16[8,72,1152]{2,1,0:T(8,128)(2,1)S(1)}, u32[]{:S(2)}, u32[]{:S(2)}) collective-permute-start(bf16[8,72,1152]{2,1,0:T(8,128)(2,1)} %collective-permute-done.4.refs_1_), channel_id=1, source_target_pairs={{0,1},{1,0},{2,3},{3,2},{4,5},{5,4},{6,7},{7,6},{8,9},{9,8},{10,11... | collective-permute-start | bytes 3981320 | tf_op jit(solution)/shard_map/ppermute | solution.py:220
  216.9 7.7 %collective-permute-start.37 = (bf16[8,144,1152]{2,1,0:T(8,128)(2,1)}, bf16[8,144,1152]{2,1,0:T(8,128)(2,1)}, u32[]{:S(2)}, u32[]{:S(2)}) collective-permute-start(bf16[8,144,1152]{2,1,0:T(8,128)(2,1)} %collective-permute-done.35.refs_1_), channel_id=1, source_target_pairs={{0,1},{1,0},{2,3},{3,2},{4,5},{5,4},{6,7},{7,6},{8,9},{9,8},{10,11... | collective-permute-start | bytes 7962632 | tf_op jit(solution)/shard_map/ppermute | solution.py:220
  224.6 18.7 %collective-permute-done.28.refs_1_ = bf16[8,72,2304]{2,1,0:T(8,128)(2,1)} collective-permute-done((bf16[8,72,2304]{2,1,0:T(8,128)(2,1)}, bf16[8,72,2304]{2,1,0:T(8,128)(2,1)}, u32[]{:S(2)}, u32[]{:S(2)}) %collective-permute-start.28) | collective-permute-done | bytes 2654240 | tf_op jit(solution)/shard_map/ppermute | solution.py:220
  243.3 9.4 %collective-permute-start.30 = (bf16[8,72,2304]{2,1,0:T(8,128)(2,1)}, bf16[8,72,2304]{2,1,0:T(8,128)(2,1)}, u32[]{:S(2)}, u32[]{:S(2)}) collective-permute-start(bf16[8,72,2304]{2,1,0:T(8,128)(2,1)} %collective-permute-done.28.refs_1_), channel_id=1, source_target_pairs={{0,1},{1,0},{2,3},{3,2},{4,5},{5,4},{6,7},{7,6},{8,9},{9,8},{10,11... | collective-permute-start | bytes 7962632 | tf_op jit(solution)/shard_map/ppermute | solution.py:220
  279.4 8.4 %assemble.9 = bf16[16,2,144,1152]{3,2,1,0:T(8,128)(2,1)} custom-call(bf16[8,144,1152]{2,1,0:T(8,128)(2,1)} %constant_dynamic-update-slice_fusion.22.refs_0_, bf16[8,144,1152]{2,1,0:T(8,128)(2,1)} %collective-permute-done.35.refs_1_, bf16[8,144,1152]{2,1,0:T(8,128)(2,1)} %collective-permute-done.36.refs_2_, bf16[8,144,1152]{2,1,0:T(8,128)(2,1)} %collective-permute-done.37.refs_3_), custom_call_target="tpu_custom_call" | custom-call | bytes 21233664 | tf_op jit(solution)/shard_map/assemble/pallas_call | solution.py:298
  287.8 8.3 %assemble.8 = bf16[16,72,4608]{2,1,0:T(8,128)(2,1)} custom-call(bf16[8,72,2304]{2,1,0:T(8,128)(2,1)} %constant_dynamic-update-slice_fusion.17.refs_0_, bf16[8,72,2304]{2,1,0:T(8,128)(2,1)} %collective-permute-done.28.refs_1_, bf16[8,72,2304]{2,1,0:T(8,128)(2,1)} %collective-permute-done.29.refs_2_, bf16[8,72,2304]{2,1,0:T(8,128)(2,1)} %collective-permute-done.30.refs_3_), custom_call_target="tpu_custom_call" | custom-call | bytes 21233664 | tf_op jit(solution)/shard_map/assemble/pallas_call | solution.py:298
  296.1 17.9 %multiply_convert_fusion.1 = (bf16[258,4608]{1,0:T(8,128)(2,1)}, f32[258,4608]{1,0:T(8,128)}, f32[258,4608]{1,0:T(8,128)}) fusion(f32[4608]{0:T(1024)S(1)} %add.823, bf16[1152,4608]{1,0:T(8,128)(2,1)} %bitcast.446, f32[258,1152]{1,0:T(8,128)S(1)} %get-tuple-element.96, f32[1152]{0:T(1024)S(1)} %add.820, f32[1152]{0:T(1024)S(1)} %mul.225, ...), kind=kOutput, calls=%fused_computation.21 | convolution fusion | flops 2819093760 | bytes 23724048 | tf_op jit(solution)/shard_map/dot_general | solution.py:492
  314.1 8.7 %convert_reduce_fusion = (f32[4608]{0:T(1024)}, bf16[258,4608]{1,0:T(8,128)(2,1)}) fusion(f32[258,4608]{1,0:T(8,128)} %get-tuple-element.35, f32[258,4608]{1,0:T(8,128)} %get-tuple-element.97, bf16[4608,1152]{1,0:T(8,128)(2,1)S(1)} %bitcast.442, bf16[258,1152]{1,0:T(8,128)(2,1)S(1)} %copy-done.23), kind=kOutput, calls=%fused_computation.19 | convolution fusion | flops 2758159872 | bytes 23118336 | tf_op jit(solution)/shard_map/rf,cf->rc/dot_general | solution.py:40
  350.1 8.6 %multiply_reduce_fusion.3 = (f32[1152]{0:T(1024)S(1)}, f32[258]{0:T(512)S(1)}, f32[1152]{0:T(1024)S(1)}, f32[258,1152]{1,0:T(8,128)}) fusion(f32[258,1152]{1,0:T(8,128)S(1)} %copy-done.4, f32[258]{0:T(512)S(1)} %copy-done.54, f32[258]{0:T(512)S(1)} %copy-done.46, f32[1152]{0:T(1024)S(1)} %mul.212, bf16[1152,3456]{1,0:T(8,128)(2,1)} %bitcast.462, ...), kind=kOutput, calls=%fused_computation.96 | convolution fusion | flops 2062082048 | bytes 12140568 | tf_op jit(solution)/shard_map/rf,cf->rc/dot_general | solution.py:40
  394.8 6.8 %convolution_convert_fusion.4 = bf16[1152,1792]{1,0:T(8,128)(2,1)} fusion(bf16[258,3456]{0,1:T(8,128)(2,1)} %pad_maximum_fusion, s32[]{:T(128)S(6)} %select_n.342, f32[258,1152]{1,0:T(8,128)S(1)} %copy-done.5, f32[1152]{0:T(1024)S(1)} %copy-done.60, f32[1152]{0:T(1024)S(1)} %mul.212, f32[258]{0:T(512)S(1)} %copy-done.55, f32[258]{0:T(512)S(1)} %copy-done.47), kind=kOutput, calls=%fused_computation.4 | convolution fusion | flops 1068772608 | bytes 6705172 | tf_op jit(solution)/shard_map/rc,rd->cd/dot_general | solution.py:44
  463.6 17.8 %collective-permute-done.45 = bf16[2,4,72,1792]{3,2,1,0:T(8,128)(2,1)S(1)} collective-permute-done((bf16[2,4,72,1792]{3,2,1,0:T(8,128)(2,1)S(1)}, bf16[2,4,72,1792]{3,2,1,0:T(8,128)(2,1)S(1)}, u32[]{:S(2)}, u32[]{:S(2)}) %collective-permute-start.45) | collective-permute-done | bytes 2064416 | tf_op jit(solution)/shard_map/ppermute | solution.py:220
  491.7 18.4 %collective-permute-done.46 = bf16[4,72,1792]{2,1,0:T(8,128)(2,1)} collective-permute-done((bf16[4,72,1792]{2,1,0:T(8,128)(2,1)}, bf16[4,72,1792]{2,1,0:T(8,128)(2,1)}, u32[]{:S(2)}, u32[]{:S(2)}) %collective-permute-start.46) | collective-permute-done | bytes 1032224 | tf_op jit(solution)/shard_map/ppermute | solution.py:220
  530.4 10.7 %collective-permute-done.48 = bf16[72,1792]{1,0:T(8,128)(2,1)} collective-permute-done((bf16[72,1792]{1,0:T(8,128)(2,1)S(1)}, bf16[72,1792]{1,0:T(8,128)(2,1)}, u32[]{:S(2)}, u32[]{:S(2)}) %collective-permute-start.48) | collective-permute-done | bytes 258080 | tf_op jit(solution)/shard_map/ppermute | solution.py:220
  558.6 9.0 %collective-permute-done.60 = bf16[4,72,2304]{2,1,0:T(8,128)(2,1)} collective-permute-done((bf16[4,72,2304]{2,1,0:T(8,128)(2,1)}, bf16[4,72,2304]{2,1,0:T(8,128)(2,1)}, u32[]{:S(2)}, u32[]{:S(2)}) %collective-permute-start.60) | collective-permute-done | bytes 1327136 | tf_op jit(solution)/shard_map/ppermute | solution.py:220
  589.0 29.7 %collective-permute-done.62 = bf16[72,2304]{1,0:T(8,128)(2,1)} collective-permute-done((bf16[72,2304]{1,0:T(8,128)(2,1)}, bf16[72,2304]{1,0:T(8,128)(2,1)}, u32[]{:S(2)}, u32[]{:S(2)}) %collective-permute-start.62) | collective-permute-done | bytes 331808 | tf_op jit(solution)/shard_map/ppermute | solution.py:220
  620.6 8.6 %collective-permute-done.69 = bf16[144,1152]{1,0:T(8,128)(2,1)S(1)} collective-permute-done((bf16[144,1152]{1,0:T(8,128)(2,1)S(1)}, bf16[144,1152]{1,0:T(8,128)(2,1)S(1)}, u32[]{:S(2)}, u32[]{:S(2)}) %collective-permute-start.69) | collective-permute-done | bytes 331808 | tf_op jit(solution)/shard_map/ppermute | solution.py:220
  (466 shorter events, 319.7 us)
Async XLA Ops:
  37.0 108.4 %collective-permute-start.8 = (f32[2,3168]{1,0:T(2,128)S(1)}, f32[2,3168]{1,0:T(2,128)S(1)}, u32[]{:S(2)}, u32[]{:S(2)}) collective-permute-start(f32[2,3168]{1,0:T(2,128)S(1)} %maximum_select_fusion.5), channel_id=1, source_target_pairs={{0,2},{1,3},{2,0},{3,1},{4,6},{5,7},{6,4},{7,5},{8,10},{9,11},{10,... | collective-permute-start | bytes 76040 | tf_op jit(solution)/shard_map/ppermute | solution.py:220
  50.5 95.6 %collective-permute-start.34 = (bf16[4,144,1152]{2,1,0:T(8,128)(2,1)S(1)}, bf16[4,144,1152]{2,1,0:T(8,128)(2,1)S(1)}, u32[]{:S(2)}, u32[]{:S(2)}) collective-permute-start(bf16[4,144,1152]{2,1,0:T(8,128)(2,1)S(1)} %pad_maximum_fusion.5), channel_id=1, source_target_pairs={{0,4},{1,3},{2,6},{3,1},{4,0},{5,7},{6,2},{7,5},{8,12},{9,11},{10,... | collective-permute-start | bytes 3981320 | tf_op jit(solution)/shard_map/ppermute | solution.py:220
  74.9 39.6 %collective-permute-start.25 = (bf16[72,2304]{1,0:T(8,128)(2,1)S(1)}, bf16[72,2304]{1,0:T(8,128)(2,1)S(1)}, u32[]{:S(2)}, u32[]{:S(2)}) collective-permute-start(bf16[72,2304]{1,0:T(8,128)(2,1)S(1)} %get-tuple-element.67), channel_id=1, source_target_pairs={{0,16},{1,17},{2,18},{3,19},{4,20},{5,21},{6,22},{7,23},{8,24},{9,... | collective-permute-start | bytes 995336 | tf_op jit(solution)/shard_map/ppermute | solution.py:220
  145.4 52.7 %collective-permute-start.14 = (bf16[8,72,1792]{2,1,0:T(8,128)(2,1)}, bf16[8,72,1792]{2,1,0:T(8,128)(2,1)}, u32[]{:S(2)}, u32[]{:S(2)}) collective-permute-start(bf16[8,72,1792]{2,1,0:T(8,128)(2,1)} %constant_dynamic-update-slice_fusion.7.refs_0_), channel_id=1, source_target_pairs={{0,2},{1,5},{2,0},{3,7},{4,6},{5,1},{6,4},{7,3},{8,10},{9,13},{10,... | collective-permute-start | bytes 6193160 | tf_op jit(solution)/shard_map/ppermute | solution.py:220
  146.1 40.4 %collective-permute-start.4 = (bf16[8,72,1152]{2,1,0:T(8,128)(2,1)S(1)}, bf16[8,72,1152]{2,1,0:T(8,128)(2,1)}, u32[]{:S(2)}, u32[]{:S(2)}) collective-permute-start(bf16[8,72,1152]{2,1,0:T(8,128)(2,1)S(1)} %constant_dynamic-update-slice_fusion.2.refs_0_), channel_id=1, source_target_pairs={{0,2},{1,5},{2,0},{3,7},{4,6},{5,1},{6,4},{7,3},{8,10},{9,13},{10,... | collective-permute-start | bytes 3981320 | tf_op jit(solution)/shard_map/ppermute | solution.py:220
  173.7 43.2 %collective-permute-start.35 = (bf16[8,144,1152]{2,1,0:T(8,128)(2,1)}, bf16[8,144,1152]{2,1,0:T(8,128)(2,1)}, u32[]{:S(2)}, u32[]{:S(2)}) collective-permute-start(bf16[8,144,1152]{2,1,0:T(8,128)(2,1)} %constant_dynamic-update-slice_fusion.22.refs_0_), channel_id=1, source_target_pairs={{0,2},{1,5},{2,0},{3,7},{4,6},{5,1},{6,4},{7,3},{8,10},{9,13},{10,... | collective-permute-start | bytes 7962632 | tf_op jit(solution)/shard_map/ppermute | solution.py:220
  173.8 69.6 %collective-permute-start.28 = (bf16[8,72,2304]{2,1,0:T(8,128)(2,1)}, bf16[8,72,2304]{2,1,0:T(8,128)(2,1)}, u32[]{:S(2)}, u32[]{:S(2)}) collective-permute-start(bf16[8,72,2304]{2,1,0:T(8,128)(2,1)} %constant_dynamic-update-slice_fusion.17.refs_0_), channel_id=1, source_target_pairs={{0,2},{1,5},{2,0},{3,7},{4,6},{5,1},{6,4},{7,3},{8,10},{9,13},{10,... | collective-permute-start | bytes 7962632 | tf_op jit(solution)/shard_map/ppermute | solution.py:220
  198.1 54.6 %collective-permute-start.16 = (bf16[8,72,1792]{2,1,0:T(8,128)(2,1)}, bf16[8,72,1792]{2,1,0:T(8,128)(2,1)}, u32[]{:S(2)}, u32[]{:S(2)}) collective-permute-start(bf16[8,72,1792]{2,1,0:T(8,128)(2,1)} %collective-permute-done.14.refs_1_), channel_id=1, source_target_pairs={{0,1},{1,0},{2,3},{3,2},{4,5},{5,4},{6,7},{7,6},{8,9},{9,8},{10,11... | collective-permute-start | bytes 6193160 | tf_op jit(solution)/shard_map/ppermute | solution.py:220
  205.3 74.0 %collective-permute-start.36 = (bf16[8,144,1152]{2,1,0:T(8,128)(2,1)}, bf16[8,144,1152]{2,1,0:T(8,128)(2,1)}, u32[]{:S(2)}, u32[]{:S(2)}) collective-permute-start(bf16[8,144,1152]{2,1,0:T(8,128)(2,1)} %constant_dynamic-update-slice_fusion.22.refs_0_), channel_id=1, source_target_pairs={{0,1},{1,0},{2,3},{3,2},{4,5},{5,4},{6,7},{7,6},{8,9},{9,8},{10,11... | collective-permute-start | bytes 7962632 | tf_op jit(solution)/shard_map/ppermute | solution.py:220
  216.7 71.0 %collective-permute-start.29 = (bf16[8,72,2304]{2,1,0:T(8,128)(2,1)}, bf16[8,72,2304]{2,1,0:T(8,128)(2,1)}, u32[]{:S(2)}, u32[]{:S(2)}) collective-permute-start(bf16[8,72,2304]{2,1,0:T(8,128)(2,1)} %constant_dynamic-update-slice_fusion.17.refs_0_), channel_id=1, source_target_pairs={{0,1},{1,0},{2,3},{3,2},{4,5},{5,4},{6,7},{7,6},{8,9},{9,8},{10,11... | collective-permute-start | bytes 7962632 | tf_op jit(solution)/shard_map/ppermute | solution.py:220
  216.9 62.5 %collective-permute-start.37 = (bf16[8,144,1152]{2,1,0:T(8,128)(2,1)}, bf16[8,144,1152]{2,1,0:T(8,128)(2,1)}, u32[]{:S(2)}, u32[]{:S(2)}) collective-permute-start(bf16[8,144,1152]{2,1,0:T(8,128)(2,1)} %collective-permute-done.35.refs_1_), channel_id=1, source_target_pairs={{0,1},{1,0},{2,3},{3,2},{4,5},{5,4},{6,7},{7,6},{8,9},{9,8},{10,11... | collective-permute-start | bytes 7962632 | tf_op jit(solution)/shard_map/ppermute | solution.py:220
  243.3 44.4 %collective-permute-start.30 = (bf16[8,72,2304]{2,1,0:T(8,128)(2,1)}, bf16[8,72,2304]{2,1,0:T(8,128)(2,1)}, u32[]{:S(2)}, u32[]{:S(2)}) collective-permute-start(bf16[8,72,2304]{2,1,0:T(8,128)(2,1)} %collective-permute-done.28.refs_1_), channel_id=1, source_target_pairs={{0,1},{1,0},{2,3},{3,2},{4,5},{5,4},{6,7},{7,6},{8,9},{9,8},{10,11... | collective-permute-start | bytes 7962632 | tf_op jit(solution)/shard_map/ppermute | solution.py:220
  380.2 50.2 %collective-permute-start.38 = (bf16[4,4,72,1152]{3,2,1,0:T(8,128)(2,1)}, bf16[4,4,72,1152]{3,2,1,0:T(8,128)(2,1)S(1)}, u32[]{:S(2)}, u32[]{:S(2)}) collective-permute-start(bf16[4,4,72,1152]{3,2,1,0:T(8,128)(2,1)} %dynamic-slice_bitcast_fusion.1), channel_id=1, source_target_pairs={{0,1},{1,0},{2,3},{3,2},{4,5},{5,4},{6,7},{7,6},{8,9},{9,8},{10,11... | collective-permute-start | bytes 7962632 | tf_op jit(solution)/shard_map/ppermute | solution.py:220
  402.1 52.9 %collective-permute-start.58 = (bf16[4,4,72,2304]{3,2,1,0:T(8,128)(2,1)}, bf16[4,4,72,2304]{3,2,1,0:T(8,128)(2,1)}, u32[]{:S(2)}, u32[]{:S(2)}) collective-permute-start(bf16[4,4,72,2304]{3,2,1,0:T(8,128)(2,1)} %bitcast.514), channel_id=1, source_target_pairs={{0,1},{1,0},{2,3},{3,2},{4,5},{5,4},{6,7},{7,6},{8,9},{9,8},{10,11... | collective-permute-start | bytes 15925256 | tf_op jit(solution)/shard_map/ppermute | solution.py:220
  402.1 59.0 %collective-permute-start.65 = (bf16[4,4,144,1152]{3,2,1,0:T(8,128)(2,1)}, bf16[4,4,144,1152]{3,2,1,0:T(8,128)(2,1)}, u32[]{:S(2)}, u32[]{:S(2)}) collective-permute-start(bf16[4,4,144,1152]{3,2,1,0:T(8,128)(2,1)} %dynamic-slice_bitcast_fusion), channel_id=1, source_target_pairs={{0,1},{1,0},{2,3},{3,2},{4,5},{5,4},{6,7},{7,6},{8,9},{9,8},{10,11... | collective-permute-start | bytes 15925256 | tf_op jit(solution)/shard_map/ppermute | solution.py:220
  443.2 38.2 %collective-permute-start.45 = (bf16[2,4,72,1792]{3,2,1,0:T(8,128)(2,1)S(1)}, bf16[2,4,72,1792]{3,2,1,0:T(8,128)(2,1)S(1)}, u32[]{:S(2)}, u32[]{:S(2)}) collective-permute-start(bf16[2,4,72,1792]{3,2,1,0:T(8,128)(2,1)S(1)} %pad_maximum_fusion.3), channel_id=1, source_target_pairs={{0,2},{1,5},{2,0},{3,7},{4,6},{5,1},{6,4},{7,3},{8,10},{9,13},{10,... | collective-permute-start | bytes 6193160 | tf_op jit(solution)/shard_map/ppermute | solution.py:220
  449.7 38.3 %collective-permute-start.75 = (f32[3168]{0:T(1024)S(1)}, f32[3168]{0:T(1024)S(1)}, u32[]{:S(2)}, u32[]{:S(2)}) collective-permute-start(f32[3168]{0:T(1024)S(1)} %add.968), channel_id=1, source_target_pairs={{0,16},{1,17},{2,18},{3,19},{4,20},{5,21},{6,22},{7,23},{8,24},{9,... | collective-permute-start | bytes 38024 | tf_op jit(solution)/shard_map/ppermute | solution.py:220
  452.2 39.5 %collective-permute-start.57 = (f32[36,640]{1,0:T(8,128)S(1)}, f32[36,640]{1,0:T(8,128)S(1)}, u32[]{:S(2)}, u32[]{:S(2)}) collective-permute-start(f32[36,640]{1,0:T(8,128)S(1)} %get-tuple-element.84), channel_id=1, source_target_pairs={{0,1},{1,0},{2,3},{3,2},{4,5},{5,4},{6,7},{7,6},{8,9},{9,8},{10,11... | collective-permute-start | bytes 276488 | tf_op jit(solution)/shard_map/ppermute | solution.py:220
  455.0 59.9 %collective-permute-start.40 = (bf16[4,72,1152]{2,1,0:T(8,128)(2,1)}, bf16[4,72,1152]{2,1,0:T(8,128)(2,1)}, u32[]{:S(2)}, u32[]{:S(2)}) collective-permute-start(bf16[4,72,1152]{2,1,0:T(8,128)(2,1)} %fusion.29), channel_id=1, source_target_pairs={{0,4},{1,3},{2,6},{3,1},{4,0},{5,7},{6,2},{7,5},{8,12},{9,11},{10,... | collective-permute-start | bytes 1990664 | tf_op jit(solution)/shard_map/ppermute | solution.py:220
  461.2 81.7 %collective-permute-start.59 = (bf16[2,4,72,2304]{3,2,1,0:T(8,128)(2,1)}, bf16[2,4,72,2304]{3,2,1,0:T(8,128)(2,1)}, u32[]{:S(2)}, u32[]{:S(2)}) collective-permute-start(bf16[2,4,72,2304]{3,2,1,0:T(8,128)(2,1)} %pad_maximum_fusion.1), channel_id=1, source_target_pairs={{0,2},{1,5},{2,0},{3,7},{4,6},{5,1},{6,4},{7,3},{8,10},{9,13},{10,... | collective-permute-start | bytes 7962632 | tf_op jit(solution)/shard_map/ppermute | solution.py:220
  488.0 61.5 %collective-permute-start.66 = (bf16[2,4,144,1152]{3,2,1,0:T(8,128)(2,1)}, bf16[2,4,144,1152]{3,2,1,0:T(8,128)(2,1)}, u32[]{:S(2)}, u32[]{:S(2)}) collective-permute-start(bf16[2,4,144,1152]{3,2,1,0:T(8,128)(2,1)} %pad_maximum_fusion.2), channel_id=1, source_target_pairs={{0,2},{1,5},{2,0},{3,7},{4,6},{5,1},{6,4},{7,3},{8,10},{9,13},{10,... | collective-permute-start | bytes 7962632 | tf_op jit(solution)/shard_map/ppermute | solution.py:220
  572.8 45.9 %collective-permute-start.62 = (bf16[72,2304]{1,0:T(8,128)(2,1)}, bf16[72,2304]{1,0:T(8,128)(2,1)}, u32[]{:S(2)}, u32[]{:S(2)}) collective-permute-start(bf16[72,2304]{1,0:T(8,128)(2,1)} %get-tuple-element.43), channel_id=1, source_target_pairs={{0,16},{1,17},{2,18},{3,19},{4,20},{5,21},{6,22},{7,23},{8,24},{9,... | collective-permute-start | bytes 995336 | tf_op jit(solution)/shard_map/ppermute | solution.py:220
  583.7 37.0 %collective-permute-start.68 = (bf16[144,1152]{1,0:T(8,128)(2,1)S(1)}, bf16[144,1152]{1,0:T(8,128)(2,1)S(1)}, u32[]{:S(2)}, u32[]{:S(2)}) collective-permute-start(bf16[144,1152]{1,0:T(8,128)(2,1)S(1)} %get-tuple-element.36), channel_id=1, source_target_pairs={{0,8},{1,9},{2,10},{3,11},{4,12},{5,13},{6,14},{7,15},{8,0},{9,1},... | collective-permute-start | bytes 995336 | tf_op jit(solution)/shard_map/ppermute | solution.py:220
  586.8 42.4 %collective-permute-start.69 = (bf16[144,1152]{1,0:T(8,128)(2,1)S(1)}, bf16[144,1152]{1,0:T(8,128)(2,1)S(1)}, u32[]{:S(2)}, u32[]{:S(2)}) collective-permute-start(bf16[144,1152]{1,0:T(8,128)(2,1)S(1)} %get-tuple-element.38), channel_id=1, source_target_pairs={{0,16},{1,17},{2,18},{3,19},{4,20},{5,21},{6,22},{7,23},{8,24},{9,... | collective-permute-start | bytes 995336 | tf_op jit(solution)/shard_map/ppermute | solution.py:220
  (125 other events, 2145.3 us)
